TPU v7x, 512 devices: a whole 4x8x8 slice. The times are simulated.
512 devices in a mesh: node: 64 (over y, z), col: 8 (over x, core).
Axes of the slice: x: 4, y: 8, z: 8, core: 2. Of those that a mesh axis runs over, the one named last changes fastest.
Arguments:
- x_t: bfloat16 [512, 32768], P('col', 'node'), may hold values from -6 to 6
- adj_tiles: bfloat16 [4096, 128, 128], P('node'), may hold values from -0.1875 to 0.1875
- tile_rows: int32 [4096], P('node'), may hold values from 0 to 3
- tile_cols: int32 [4096], P('node'), may hold values from 0 to 255, as said below
- tile_counts: int32 [64], P('node'), may hold values from 8 to 64, as said below
- w_first: bfloat16 [512, 512], P('col'), may hold values from -0.25 to 0.25
- b_first: float32 [512], P('col'), may hold values from -3 to 3
- w_second: bfloat16 [512, 512], P('col'), may hold values from -0.25 to 0.25
- b_second: float32 [512], P('col'), may hold values from -3 to 3
Outputs:
- out_t: float32 [512, 32768], P('col', 'node')
Inputs may be any that keep to these rules, and one draw needn't show every extreme that they name: `tile_cols`: column blocks q * 4 to q * 4 + 3 belong to device q of node. Among the live tiles of one device, at most 2 distinct column blocks belong to any one device, and every device's first 2 tiles name 2 distinct blocks of one device. `tile_counts`: some device has all 64 slots live.
All inputs are finite; a program needn't handle non-finite values.
Results may differ from a plain program's by a relative error of at most 0.004.
Values may be sent and summed in bfloat16 or wider, within the bound.
A program may use at most 64 MiB of HBM per device.

v0:
```python
import jax
import jax.numpy as jnp
from jax import lax
from jax.sharding import PartitionSpec as P

BLK = 128
CAP = 2


def tile_sum(x_blocks, tile_values, selector):
    products = jnp.einsum("fnj,nij->fni", x_blocks, tile_values, preferred_element_type=jnp.float32)
    return jnp.einsum("fni,nb->fbi", products, selector, precision=lax.Precision.HIGHEST)


def aggregate(feat_t, adj_tiles, tile_rows, live_count, plan):
    feat_local = feat_t.shape[0]
    row_blocks = feat_t.shape[1] // BLK
    tile_total = adj_tiles.shape[0]
    asked_of, tile_slot = plan
    own_blocks = feat_t.reshape(feat_local, row_blocks, BLK)
    outgoing = jnp.take(own_blocks, asked_of.reshape(-1), axis=1)
    incoming = lax.all_to_all(outgoing, "node", split_axis=1, concat_axis=1, tiled=True)
    x_blocks = jnp.take(incoming, tile_slot, axis=1)
    is_live = jnp.arange(tile_total, dtype=jnp.int32) < live_count
    selector = (
        (tile_rows[:, None] == jnp.arange(row_blocks, dtype=jnp.int32)[None, :]) & is_live[:, None]
    ).astype(jnp.float32)
    summed = tile_sum(x_blocks, adj_tiles, selector)
    return summed.reshape(feat_local, row_blocks * BLK).astype(jnp.bfloat16)


def dense_layer(aggregated, weight_local, bias_local):
    summed = jnp.dot(
        weight_local,
        lax.all_gather(aggregated, "col", axis=0, tiled=True),
        preferred_element_type=jnp.float32,
    )
    return summed + bias_local[:, None]


def body(x_t, adj_tiles, tile_rows, tile_cols, tile_counts, w_first, b_first, w_second, b_second):
    row_blocks = x_t.shape[1] // BLK
    peer_count = lax.axis_size("node")
    block_total = peer_count * row_blocks
    live_count = tile_counts[0]
    is_live = jnp.arange(tile_cols.shape[0], dtype=jnp.int32) < live_count
    named = (tile_cols[:, None] == jnp.arange(block_total, dtype=jnp.int32)[None, :]) & is_live[
        :, None
    ]
    needed = jnp.any(named, axis=0).astype(jnp.int32).reshape(peer_count, row_blocks)
    position = jnp.cumsum(needed, axis=1) - 1
    slot_hit = (needed[:, :, None] == 1) & (
        position[:, :, None] == jnp.arange(CAP, dtype=jnp.int32)[None, None, :]
    )
    wanted = jnp.sum(
        slot_hit.astype(jnp.int32) * jnp.arange(row_blocks, dtype=jnp.int32)[None, :, None], axis=1
    )
    asked_of = lax.all_to_all(wanted, "node", split_axis=0, concat_axis=0, tiled=True)
    owner_base = (jnp.arange(peer_count, dtype=jnp.int32) * CAP)[:, None]
    slot_table = (owner_base + jnp.clip(position, 0, CAP - 1)).reshape(-1)
    tile_slot = jnp.take(slot_table, tile_cols)
    plan = (asked_of, tile_slot)
    y_first = aggregate(x_t, adj_tiles, tile_rows, live_count, plan)
    h_first = jnp.maximum(dense_layer(y_first, w_first, b_first), 0.0).astype(jnp.bfloat16)
    y_second = aggregate(h_first, adj_tiles, tile_rows, live_count, plan)
    return dense_layer(y_second, w_second, b_second)


def solution(mesh):
    return jax.shard_map(
        body,
        mesh=mesh,
        in_specs=(
            P("col", "node"),
            P("node", None, None),
            P("node"),
            P("node"),
            P("node"),
            P("col", None),
            P("col"),
            P("col", None),
            P("col"),
        ),
        out_specs=P("col", "node"),
        check_vma=False,
    )
```

profile of v0, /device:TPU:25, one launch (start us, length us, event | category | flops | bytes accessed | tf_op | source)
XLA Modules:
  0.0 206.9 jit_solution(1067784979185888805)
XLA Ops:
  0.8 0.8 fusion.23
  1.6 0.1 reshape.72
  1.7 0.1 copy.23
  1.8 0.2 reduce_window_sum.11
  2.0 0.1 clamp_add_fusion
  2.1 0.1 copy.24
  2.2 0.7 copy.25
  2.9 15.8 %all-to-all-start = ((s32[64,1,2]{2,1,0:T(1,128)}), s32[64,1,2]{2,1,0:T(1,128)S(1)}, u32[]{:S(2)}, u32[]{:S(2)}) async-start(s32[64,1,2]{2,1,0:T(1,128)} %copy.25), calls=%async_computation | async-start | bytes 65536 | tf_op jit(solution)/shard_map/all_to_all | solution.py:58
  18.7 0.9 copy_bitcast_fusion.3
  19.6 7.5 %all-to-all-done = s32[64,1,2]{2,1,0:T(1,128)S(1)} async-done(((s32[64,1,2]{2,1,0:T(1,128)}), s32[64,1,2]{2,1,0:T(1,128)S(1)}, u32[]{:S(2)}, u32[]{:S(2)}) %all-to-all-start) | async-done | bytes 544 | tf_op jit(solution)/shard_map/all_to_all | solution.py:58
  27.1 0.5 broadcast.114
  27.6 0.7 reduce.3
  28.3 0.1 reshape.70
  28.5 2.1 %gather_fusion.1 = bf16[128,64,128]{2,1,0:T(8,128)(2,1)} fusion(bf16[64,4,128]{2,0,1:T(8,128)(2,1)S(1)} %copy_bitcast_fusion.3, s32[1024]{0:T(1024)S(1)} %pad_clamp_fusion.1), kind=kCustom, calls=%fused_computation.clone | custom fusion | bytes 4194816 | tf_op jit(solution)/shard_map/jit(_take)/gather | solution.py:21
  30.6 3.2 %select_bitcast_fusion.1 = bf16[64,128,128]{2,0,1:T(8,128)(2,1)} fusion(bf16[128,64,128]{2,1,0:T(8,128)(2,1)} %gather_fusion.1, pred[128]{0:T(512)(128)(4,1)S(1)} %compare_and_fusion.1), kind=kLoop, calls=%fused_computation.10 | loop fusion | flops 1048576 | bytes 4194432 | tf_op jit(solution)/shard_map/jit(_take)/select_n | solution.py:21
  33.8 8.0 %all-to-all-start.1 = ((bf16[64,128,128]{2,0,1:T(8,128)(2,1)}), bf16[64,128,128]{2,0,1:T(8,128)(2,1)}, u32[]{:S(2)}, u32[]{:S(2)}) async-start(bf16[64,128,128]{2,0,1:T(8,128)(2,1)} %select_bitcast_fusion.1), calls=%async_computation.1 | async-start | bytes 4194304 | tf_op jit(solution)/shard_map/all_to_all | solution.py:22
  41.8 0.1 add.63
  42.0 0.8 gather_fusion
  42.8 53.7 %all-to-all-done.1 = bf16[64,128,128]{2,0,1:T(8,128)(2,1)} async-done(((bf16[64,128,128]{2,0,1:T(8,128)(2,1)}), bf16[64,128,128]{2,0,1:T(8,128)(2,1)}, u32[]{:S(2)}, u32[]{:S(2)}) %all-to-all-start.1) | async-done | bytes 2097184 | tf_op jit(solution)/shard_map/all_to_all | solution.py:22
  96.5 2.3 %gather_fusion.2 = bf16[64,64,128]{2,1,0:T(8,128)(2,1)S(1)} fusion(bf16[64,128,128]{2,0,1:T(8,128)(2,1)} %all-to-all-done.1, s32[1024]{0:T(1024)S(1)} %pad_clamp_fusion), kind=kCustom, calls=%fused_computation.1.clone | custom fusion | bytes 2097408 | tf_op jit(solution)/shard_map/jit(_take)/gather | solution.py:23
  98.8 1.5 convolution_bitcast_fusion.1
  100.4 2.0 fusion.7
  102.4 15.1 %all_gather.6 = bf16[512,512]{1,0:T(8,128)(2,1)S(1)} all-gather(bf16[64,512]{1,0:T(8,128)(2,1)S(1)} %bitcast.53), channel_id=1, replica_groups=mesh['node'=64,'col'=8] {'col'}, dimensions={0}, use_global_device_ids=true | all-gather | bytes 589824 | tf_op jit(solution)/shard_map/all_gather | solution.py:35
  117.5 0.2 fusion.13
  117.7 2.2 %gather_fusion.3 = bf16[128,64,128]{2,1,0:T(8,128)(2,1)} fusion(bf16[64,4,128]{2,0,1:T(8,128)(2,1)S(1)} %bitcast.50, s32[1024]{0:T(1024)S(1)} %pad_clamp_fusion.1), kind=kCustom, calls=%fused_computation.2.clone | custom fusion | bytes 4194816 | tf_op jit(solution)/shard_map/jit(_take)/gather | solution.py:21
  119.9 1.9 select_bitcast_fusion
  121.7 62.4 %all_to_all.19 = bf16[64,128,128]{2,0,1:T(8,128)(2,1)} all-to-all(bf16[64,128,128]{2,0,1:T(8,128)(2,1)S(1)} %select_bitcast_fusion), channel_id=1, replica_groups=mesh['node'=64,'col'=8] {'node'}, dimensions={1} | all-to-all | bytes 4194304 | tf_op jit(solution)/shard_map/all_to_all | solution.py:22
  184.1 2.3 %gather_fusion.4 = bf16[64,64,128]{2,1,0:T(8,128)(2,1)S(1)} fusion(bf16[64,128,128]{2,0,1:T(8,128)(2,1)} %all_to_all.19, s32[1024]{0:T(1024)S(1)} %pad_clamp_fusion), kind=kCustom, calls=%fused_computation.3.clone | custom fusion | bytes 2097408 | tf_op jit(solution)/shard_map/jit(_take)/gather | solution.py:23
  186.4 1.5 convolution_bitcast_fusion
  188.0 2.0 fusion.10
  190.0 16.0 %all_gather.7 = bf16[512,512]{1,0:T(8,128)(2,1)S(1)} all-gather(bf16[64,512]{1,0:T(8,128)(2,1)S(1)} %bitcast.54), channel_id=1, replica_groups=mesh['node'=64,'col'=8] {'col'}, dimensions={0}, use_global_device_ids=true | all-gather | bytes 589824 | tf_op jit(solution)/shard_map/all_gather | solution.py:35
  206.0 0.9 fusion.4
  (29 shorter events, 0.2 us)
Async XLA Ops:
  0.0 98.8 %copy-start = (bf16[64,128,128]{2,1,0:T(8,128)(2,1)S(1)}, bf16[64,128,128]{2,1,0:T(8,128)(2,1)}, u32[]{:S(2)}) copy-start(bf16[64,128,128]{2,1,0:T(8,128)(2,1)} %param.14) | copy-start | bytes 6291460
  2.9 24.2 %all-to-all-start = ((s32[64,1,2]{2,1,0:T(1,128)}), s32[64,1,2]{2,1,0:T(1,128)S(1)}, u32[]{:S(2)}, u32[]{:S(2)}) async-start(s32[64,1,2]{2,1,0:T(1,128)} %copy.25), calls=%async_computation | async-start | bytes 65536 | tf_op jit(solution)/shard_map/all_to_all | solution.py:58
  33.8 8.1 %copy-start.5 = (s32[64]{0:T(128)S(1)}, s32[64]{0:T(128)}, u32[]{:S(2)}) copy-start(s32[64]{0:T(128)} %param.16) | copy-start | bytes 772
  33.8 62.7 %all-to-all-start.1 = ((bf16[64,128,128]{2,0,1:T(8,128)(2,1)}), bf16[64,128,128]{2,0,1:T(8,128)(2,1)}, u32[]{:S(2)}, u32[]{:S(2)}) async-start(bf16[64,128,128]{2,0,1:T(8,128)(2,1)} %select_bitcast_fusion.1), calls=%async_computation.1 | async-start | bytes 4194304 | tf_op jit(solution)/shard_map/all_to_all | solution.py:22
  98.8 1.6 copy-start.3
  100.4 17.1 %copy-start.1 = (bf16[64,512]{1,0:T(8,128)(2,1)S(1)}, bf16[64,512]{1,0:T(8,128)(2,1)}, u32[]{:S(2)}) copy-start(bf16[64,512]{1,0:T(8,128)(2,1)} %param.18) | copy-start | bytes 196612
  100.4 17.1 %copy-start.6 = (f32[64]{0:T(128)S(1)}, f32[64]{0:T(128)}, u32[]{:S(2)}) copy-start(f32[64]{0:T(128)} %param.19) | copy-start | bytes 772
  188.0 18.1 %copy-start.2 = (bf16[64,512]{1,0:T(8,128)(2,1)S(1)}, bf16[64,512]{1,0:T(8,128)(2,1)}, u32[]{:S(2)}) copy-start(bf16[64,512]{1,0:T(8,128)(2,1)} %param.20) | copy-start | bytes 196612
  188.0 18.0 %copy-start.4 = (f32[64]{0:T(128)S(1)}, f32[64]{0:T(128)}, u32[]{:S(2)}) copy-start(f32[64]{0:T(128)} %param.21) | copy-start | bytes 772
where the time goes:
time: 207 us
  blocking collectives  93.5 us (45%)
  waiting for transfers between devices  61.2 us (30%)
  starting transfers between devices  23.9 us (12%)
  local copies, waits for them, and re-layouts  12.4 us (6%)
  matrix products  8.07 us (4%)
  other arithmetic  6.84 us (3%)
    all_to_all x1, blocking collectives, aggregate(): lax.all_to_all(outgoing, 'node', split_axis=1, concat_axis=1, tiled=True)  62.4 us
    all_to_all x1, waiting for transfers between devices, aggregate(): lax.all_to_all(outgoing, 'node', split_axis=1, concat_axis=1, tiled=True)  53.7 us
    all_gather x2, blocking collectives, dense_layer(): lax.all_gather(aggregated, 'col', axis=0, tiled=True)  31.1 us
    all_to_all x1, starting transfers between devices, body(): lax.all_to_all(wanted, 'node', split_axis=0, concat_axis=0, tiled=True)  15.8 us
    all_to_all x1, starting transfers between devices, aggregate(): lax.all_to_all(outgoing, 'node', split_axis=1, concat_axis=1, tiled=True)  8.02 us
    all_to_all x1, waiting for transfers between devices, body(): lax.all_to_all(wanted, 'node', split_axis=0, concat_axis=0, tiled=True)  7.51 us
    select_n x3, other arithmetic, aggregate(): outgoing = jnp.take(own_blocks, asked_of.reshape(-1), axis=1)  5.01 us
    gather x2, local copies, waits for them, and re-layouts, aggregate(): x_blocks = jnp.take(incoming, tile_slot, axis=1)  4.68 us
  transfers between devices with their start and end apart: 2, of which 2 were waited for; matrix products, arithmetic and copies ran while one was open for 1% of the time, Pallas kernels for 0%

commit v1 on v0

--- a/solution.py
+++ b/solution.py
@@ -19,7 +19,10 @@
     asked_of, tile_slot = plan
     own_blocks = feat_t.reshape(feat_local, row_blocks, BLK)
     outgoing = jnp.take(own_blocks, asked_of.reshape(-1), axis=1)
-    incoming = lax.all_to_all(outgoing, "node", split_axis=1, concat_axis=1, tiled=True)
+    incoming = jnp.concatenate(
+        lax.all_to_all(jnp.stack(jnp.split(outgoing, lax.axis_size("node"), axis=1)), "node", 0, 0),
+        axis=1,
+    )
     x_blocks = jnp.take(incoming, tile_slot, axis=1)
     is_live = jnp.arange(tile_total, dtype=jnp.int32) < live_count
     selector = (

time: 207 us -> 246 us (1.19)
  local copies, waits for them, and re-layouts: 12.4 us -> 52.4 us
    unnamed x16 -> x142, local copies, waits for them, and re-layouts: 0.06 us -> 39.3 us
where the time goes in v1:
time: 246 us
  blocking collectives  93.4 us (38%)
  waiting for transfers between devices  60.6 us (25%)
  local copies, waits for them, and re-layouts  52.4 us (21%)
  starting transfers between devices  23.9 us (10%)
  matrix products  8.07 us (3%)
  other arithmetic  6.18 us (3%)
    all_to_all x1, blocking collectives, aggregate(): lax.all_to_all(jnp.stack(jnp.split(outgoing, lax.axis_size('node'), axis=...  62.2 us
    all_to_all x1, waiting for transfers between devices, aggregate(): lax.all_to_all(jnp.stack(jnp.split(outgoing, lax.axis_size('node'), axis=...  53.7 us
    unnamed x142, local copies, waits for them, and re-layouts  39.3 us
    all_gather x2, blocking collectives, dense_layer(): lax.all_gather(aggregated, 'col', axis=0, tiled=True)  31.3 us
    all_to_all x1, starting transfers between devices, body(): lax.all_to_all(wanted, 'node', split_axis=0, concat_axis=0, tiled=True)  15.8 us
    all_to_all x1, starting transfers between devices, aggregate(): lax.all_to_all(jnp.stack(jnp.split(outgoing, lax.axis_size('node'), axis=...  8.02 us
    all_to_all x1, waiting for transfers between devices, body(): lax.all_to_all(wanted, 'node', split_axis=0, concat_axis=0, tiled=True)  6.85 us
  transfers between devices with their start and end apart: 2, of which 2 were waited for; matrix products, arithmetic and copies ran while one was open for 1% of the time, Pallas kernels for 0%

profile of v1, /device:TPU:25, one launch (start us, length us, event | category | flops | bytes accessed | tf_op | source)
XLA Modules:
  0.0 245.8 jit_solution(7650705404028262723)
XLA Ops:
  0.8 0.8 fusion.23
  2.2 0.7 copy.25
  2.9 15.8 %all-to-all-start = ((s32[64,1,2]{2,1,0:T(1,128)}), s32[64,1,2]{2,1,0:T(1,128)S(1)}, u32[]{:S(2)}, u32[]{:S(2)}) async-start(s32[64,1,2]{2,1,0:T(1,128)} %copy.25), calls=%async_computation | async-start | bytes 65536 | tf_op jit(solution)/shard_map/all_to_all | solution.py:61
  18.7 0.9 copy_bitcast_fusion.3
  19.6 0.7 compare_select_fusion.2
  20.2 6.9 %all-to-all-done = s32[64,1,2]{2,1,0:T(1,128)S(1)} async-done(((s32[64,1,2]{2,1,0:T(1,128)}), s32[64,1,2]{2,1,0:T(1,128)S(1)}, u32[]{:S(2)}, u32[]{:S(2)}) %all-to-all-start) | async-done | bytes 544 | tf_op jit(solution)/shard_map/all_to_all | solution.py:61
  27.6 0.7 reduce.3
  28.5 2.2 gather_fusion.1
  30.7 1.9 select_bitcast_fusion.1
  45.4 0.6 constant_dynamic-update-slice_fusion.42
  54.0 0.6 constant_dynamic-update-slice_fusion.28
  58.9 0.6 constant_dynamic-update-slice_fusion.20
  61.3 0.6 constant_dynamic-update-slice_fusion.16
  62.0 0.6 constant_dynamic-update-slice_fusion.15
  63.8 0.6 constant_dynamic-update-slice_fusion.12
  68.7 0.6 constant_dynamic-update-slice_fusion.4
  71.1 0.6 constant_dynamic-update-slice_fusion
  71.8 8.0 %all-to-all-start.1 = ((bf16[64,64,2,128]{3,1,2,0:T(8,128)(2,1)}), bf16[64,64,2,128]{3,1,2,0:T(8,128)(2,1)}, u32[]{:S(2)}, u32[]{:S(2)}) async-start(bf16[64,64,2,128]{3,1,2,0:T(8,128)(2,1)} %constant_dynamic-update-slice_fusion), calls=%async_computation.1 | async-start | bytes 4194304 | tf_op jit(solution)/shard_map/all_to_all | solution.py:23
  79.9 0.8 gather_fusion
  80.7 53.7 %all-to-all-done.1 = bf16[64,64,2,128]{3,1,2,0:T(8,128)(2,1)} async-done(((bf16[64,64,2,128]{3,1,2,0:T(8,128)(2,1)}), bf16[64,64,2,128]{3,1,2,0:T(8,128)(2,1)}, u32[]{:S(2)}, u32[]{:S(2)}) %all-to-all-start.1) | async-done | bytes 2097184 | tf_op jit(solution)/shard_map/all_to_all | solution.py:23
  134.5 2.3 gather_fusion.2
  136.8 1.5 convolution_bitcast_fusion.1
  138.4 2.0 fusion.7
  140.4 15.1 %all_gather.6 = bf16[512,512]{1,0:T(8,128)(2,1)S(1)} all-gather(bf16[64,512]{1,0:T(8,128)(2,1)S(1)} %bitcast.572), channel_id=1, replica_groups=mesh['node'=64,'col'=8] {'col'}, dimensions={0}, use_global_device_ids=true | all-gather | bytes 589824 | tf_op jit(solution)/shard_map/all_gather | solution.py:38
  155.7 2.2 gather_fusion.3
  157.9 1.9 select_bitcast_fusion
  160.7 62.2 %all_to_all.19 = bf16[64,64,2,128]{3,1,2,0:T(8,128)(2,1)} all-to-all(bf16[64,64,2,128]{3,1,2,0:T(8,128)(2,1)S(1)} %constant_dynamic-update-slice_fusion.64), channel_id=1, replica_groups=mesh['node'=64,'col'=8] {'node'}, dimensions={0} | all-to-all | bytes 4194304 | tf_op jit(solution)/shard_map/all_to_all | solution.py:23
  222.9 2.3 gather_fusion.4
  225.2 1.5 convolution_bitcast_fusion
  226.8 2.0 fusion.10
  228.8 16.2 %all_gather.7 = bf16[512,512]{1,0:T(8,128)(2,1)S(1)} all-gather(bf16[64,512]{1,0:T(8,128)(2,1)S(1)} %bitcast.573), channel_id=1, replica_groups=mesh['node'=64,'col'=8] {'col'}, dimensions={0}, use_global_device_ids=true | all-gather | bytes 589824 | tf_op jit(solution)/shard_map/all_gather | solution.py:38
  245.0 0.9 fusion.4
  (156 shorter events, 36.6 us)
Async XLA Ops:
  0.0 136.8 %copy-start = (bf16[64,128,128]{2,1,0:T(8,128)(2,1)S(1)}, bf16[64,128,128]{2,1,0:T(8,128)(2,1)}, u32[]{:S(2)}) copy-start(bf16[64,128,128]{2,1,0:T(8,128)(2,1)} %param.14) | copy-start | bytes 6291460
  2.9 24.2 %all-to-all-start = ((s32[64,1,2]{2,1,0:T(1,128)}), s32[64,1,2]{2,1,0:T(1,128)S(1)}, u32[]{:S(2)}, u32[]{:S(2)}) async-start(s32[64,1,2]{2,1,0:T(1,128)} %copy.25), calls=%async_computation | async-start | bytes 65536 | tf_op jit(solution)/shard_map/all_to_all | solution.py:61
  71.8 8.9 %copy-start.5 = (s32[64]{0:T(128)S(1)}, s32[64]{0:T(128)}, u32[]{:S(2)}) copy-start(s32[64]{0:T(128)} %param.16) | copy-start | bytes 772
  71.8 62.7 %all-to-all-start.1 = ((bf16[64,64,2,128]{3,1,2,0:T(8,128)(2,1)}), bf16[64,64,2,128]{3,1,2,0:T(8,128)(2,1)}, u32[]{:S(2)}, u32[]{:S(2)}) async-start(bf16[64,64,2,128]{3,1,2,0:T(8,128)(2,1)} %constant_dynamic-update-slice_fusion), calls=%async_computation.1 | async-start | bytes 4194304 | tf_op jit(solution)/shard_map/all_to_all | solution.py:23
  136.8 1.6 copy-start.3
  138.4 17.1 %copy-start.1 = (bf16[64,512]{1,0:T(8,128)(2,1)S(1)}, bf16[64,512]{1,0:T(8,128)(2,1)}, u32[]{:S(2)}) copy-start(bf16[64,512]{1,0:T(8,128)(2,1)} %param.18) | copy-start | bytes 196612
  138.4 17.1 %copy-start.6 = (f32[64]{0:T(128)S(1)}, f32[64]{0:T(128)}, u32[]{:S(2)}) copy-start(f32[64]{0:T(128)} %param.19) | copy-start | bytes 772
  226.8 18.2 %copy-start.2 = (bf16[64,512]{1,0:T(8,128)(2,1)S(1)}, bf16[64,512]{1,0:T(8,128)(2,1)}, u32[]{:S(2)}) copy-start(bf16[64,512]{1,0:T(8,128)(2,1)} %param.20) | copy-start | bytes 196612
  226.8 18.2 %copy-start.4 = (f32[64]{0:T(128)S(1)}, f32[64]{0:T(128)}, u32[]{:S(2)}) copy-start(f32[64]{0:T(128)} %param.21) | copy-start | bytes 772
